TPU v7x, 256 devices: a whole 4x4x8 slice. The times are simulated.
256 devices in a mesh: ctx: 32 (over y, x, core), head: 8 (over z).
Axes of the slice: x: 4, y: 4, z: 8, core: 2. Of those that a mesh axis runs over, the one named last changes fastest.
Arguments:
- queries: float32 [16384, 8192], P('ctx', 'head'), as said below
- keys: float32 [16384, 8192], P('ctx', 'head')
- values: float32 [16384, 8192], P('ctx', 'head')
- head_gain: float32 [2, 64], P(None, 'head'), may hold values from 0.3 to 3
Outputs:
- mixed: float32 [16384, 8192], P('ctx', 'head')
Inputs may be any that keep to these rules, and one draw needn't show every extreme that they name: queries, keys and values are finite real numbers.
All inputs are finite; a program needn't handle non-finite values.
Results may differ from a plain program's by a relative error of at most 0.0003.
Values sent between devices are 32-bit elements; how exact they have to be, the bound alone decides.
A program may use at most 64 MiB of HBM per device.

v0:
```python
import math

import jax
import jax.numpy as jnp
from jax import lax
from jax.sharding import PartitionSpec as P

HEADS = 64
HD = 128
WINDOW = 128


def shifted(block, axis, distance):
    devices = range(lax.axis_size(axis))
    route = [(i - distance, i) for i in devices if i - distance in devices]
    return lax.ppermute(block, axis, route)


def swapped(block, axis, stride):
    count = lax.axis_size(axis)
    route = []
    for low in range(count):
        high = low | 1 << stride
        if high != low and high < count:
            route += [(low, high), (high, low)]
    return lax.ppermute(block, axis, route)


def shards(queries, keys, values, head_gain):
    row_count = queries.shape[0]
    head_count = head_gain.shape[1]
    head_width = queries.shape[1] // head_count
    factor = 1.0 / math.sqrt(head_width)
    highest = lax.Precision.HIGHEST
    ctx_index = lax.axis_index("ctx")
    tail_keys, tail_values = shifted(
        (keys[row_count - WINDOW :], values[row_count - WINDOW :]), "ctx", 1
    )

    def split_heads(matrix):
        return matrix.reshape(matrix.shape[0], head_count, head_width).transpose(1, 0, 2)

    query_heads = split_heads(queries)
    key_heads = split_heads(keys)
    value_heads = split_heads(values)
    block_size = math.gcd(row_count, 128)
    block_count = row_count // block_size
    query_blocks = query_heads.reshape(head_count, block_count, block_size, head_width)
    key_blocks = key_heads.reshape(head_count, block_count, block_size, head_width)
    value_blocks = value_heads.reshape(head_count, block_count, block_size, head_width)
    block_states = jnp.einsum("hnkd,hnke->hnde", key_blocks, value_blocks, precision=highest)
    local_total = jnp.sum(block_states, axis=1)
    zero_state = jnp.zeros_like(local_total)
    running = local_total
    earlier = zero_state
    for bit_number in range(lax.axis_size("ctx").bit_length() - 1):
        partner = swapped(running, "ctx", bit_number)
        upper_half = jnp.right_shift(ctx_index, bit_number) % 2 == 1
        earlier = earlier + jnp.where(upper_half, partner, 0.0)
        running = running + partner
    block_prefix = jnp.cumsum(block_states, axis=1) - block_states + earlier[:, None]
    positions = jnp.arange(block_size)
    causal = positions[:, None] >= positions[None, :]
    inner_dot = jnp.einsum("hnqd,hnkd->hnqk", query_blocks, key_blocks, precision=highest)
    inner_dot = jnp.where(causal[None, None], inner_dot, 0.0)
    linear_out = jnp.einsum("hnqk,hnke->hnqe", inner_dot, value_blocks, precision=highest)
    linear_out = linear_out + jnp.einsum(
        "hnqd,hnde->hnqe", query_blocks, block_prefix, precision=highest
    )
    linear_out = linear_out.reshape(head_count, row_count, head_width)
    window_count = row_count // WINDOW
    key_window = split_heads(jnp.concatenate([tail_keys, keys], axis=0))
    value_window = split_heads(jnp.concatenate([tail_values, values], axis=0))
    query_tiles = query_heads.reshape(head_count, window_count, WINDOW, head_width)
    key_now = key_heads.reshape(head_count, window_count, WINDOW, head_width)
    value_now = value_heads.reshape(head_count, window_count, WINDOW, head_width)
    key_prev = key_window[:, :row_count].reshape(head_count, window_count, WINDOW, head_width)
    value_prev = value_window[:, :row_count].reshape(head_count, window_count, WINDOW, head_width)
    key_both = jnp.concatenate([key_prev, key_now], axis=2)
    value_both = jnp.concatenate([value_prev, value_now], axis=2)
    scores = jnp.einsum("hnqd,hnkd->hnqk", query_tiles, key_both, precision=highest) * factor
    query_pos = jnp.arange(WINDOW)
    key_pos = jnp.arange(2 * WINDOW) - WINDOW
    spacing = query_pos[:, None] - key_pos[None, :]
    inside = (spacing >= 0) & (spacing < WINDOW)
    tile_ids = jnp.arange(window_count)
    reachable = (tile_ids[:, None] > 0) | (ctx_index > 0) | (key_pos >= 0)[None, :]
    allowed = inside[None, :, :] & reachable[:, None, :]
    scores = jnp.where(allowed[None], scores, -jnp.inf)
    biggest = jnp.max(scores, axis=-1, keepdims=True)
    weights = jnp.exp(scores - biggest)
    window_out = jnp.einsum("hnqk,hnkd->hnqd", weights, value_both, precision=highest) / jnp.sum(
        weights, axis=-1, keepdims=True
    )
    window_out = window_out.reshape(head_count, row_count, head_width)
    branch_a = window_out * head_gain[0][:, None, None]
    branch_b = linear_out * head_gain[1][:, None, None]
    square_a = jnp.sum(branch_a * branch_a, axis=(0, 2))
    square_b = jnp.sum(branch_b * branch_b, axis=(0, 2))
    square_a, square_b = lax.psum((square_a, square_b), "head")
    norm_a = jnp.sqrt(square_a / (HEADS * HD) + 1e-06)
    norm_b = jnp.sqrt(square_b / (HEADS * HD) + 1e-06)
    mixed = branch_a / norm_a[None, :, None] + branch_b / norm_b[None, :, None]
    return mixed.transpose(1, 0, 2).reshape(row_count, head_count * head_width)


def solution(mesh):
    in_specs = (P("ctx", "head"), P("ctx", "head"), P("ctx", "head"), P(None, "head"))
    out_specs = P("ctx", "head")
    return jax.shard_map(shards, mesh=mesh, in_specs=in_specs, out_specs=out_specs, check_vma=False)
```

profile of v0, /device:TPU:8, one launch (start us, length us, event | category | flops | bytes accessed | tf_op | source)
XLA Modules:
  0.0 116.7 jit_solution(10032017527552223770)
XLA Ops:
  0.0 1.9 %copy_bitcast_fusion.1 = f32[512,8,128]{2,0,1:T(8,128)S(1)} fusion(f32[512,1024]{1,0:T(8,128)} %param.6), kind=kLoop, calls=%fused_computation.17 | loop fusion | bytes 4194304 | tf_op jit(solution)/shard_map/reshape | solution.py:41
  2.7 0.5 copy-done.2
  3.2 5.1 %fusion.38 = (f32[8,128,128]{2,1,0:T(8,128)S(1)}, f32[8,4,128,128]{3,2,1,0:T(8,128)}) fusion(f32[8,4,128,128]{3,2,1,0:T(8,128)S(1)} %bitcast.91, f32[8,4,128,128]{3,0,2,1:T(8,128)S(1)} %bitcast.97), kind=kOutput, calls=%fused_computation.61 | convolution fusion | flops 805699584 | bytes 6815744 | tf_op jit(solution)/shard_map/hnkd,hnke->hnde/dot_general | solution.py:51
  8.3 0.9 slice.18
  9.2 2.4 %collective-permute-start = (f32[128,1024]{1,0:T(8,128)}, f32[128,1024]{1,0:T(8,128)}, u32[]{:S(2)}, u32[]{:S(2)}) collective-permute-start(f32[128,1024]{1,0:T(8,128)} %slice.18), channel_id=1, source_target_pairs={{0,8},{8,16},{16,24},{24,32},{32,40},{40,48},{48,56},{56,64},{64,7... | collective-permute-start | bytes 1572872 | tf_op jit(solution)/shard_map/ppermute | solution.py:16
  11.5 1.9 %slice.20 = f32[128,1024]{1,0:T(8,128)} slice(f32[512,1024]{1,0:T(8,128)} %param.6), slice={[384:512], [0:1024]} | slice | bytes 1048576 | tf_op jit(solution)/shard_map/slice | solution.py:37
  13.4 3.0 %collective-permute-start.1 = (f32[128,1024]{1,0:T(8,128)}, f32[128,1024]{1,0:T(8,128)}, u32[]{:S(2)}, u32[]{:S(2)}) collective-permute-start(f32[128,1024]{1,0:T(8,128)} %slice.20), channel_id=1, source_target_pairs={{0,8},{8,16},{16,24},{24,32},{32,40},{40,48},{48,56},{56,64},{64,7... | collective-permute-start | bytes 1572872 | tf_op jit(solution)/shard_map/ppermute | solution.py:16
  16.5 1.5 %copy_bitcast_fusion.2 = f32[512,8,128]{2,0,1:T(8,128)} fusion(f32[512,1024]{1,0:T(8,128)S(1)} %copy-done), kind=kLoop, calls=%fused_computation.18 | loop fusion | bytes 4194304 | tf_op jit(solution)/shard_map/reshape | solution.py:41
  18.0 2.1 %copy.22 = f32[64,8,8,128]{3,2,1,0:T(8,128)S(1)} copy(f32[64,8,8,128]{3,1,2,0:T(8,128)} %bitcast.100) | data formatting | bytes 4194304
  20.5 1.2 %copy-done.5 = f32[8,4,128,128]{3,2,1,0:T(8,128)S(1)} copy-done((f32[8,4,128,128]{3,2,1,0:T(8,128)S(1)}, f32[8,4,128,128]{3,2,1,0:T(8,128)}, u32[]{:S(2)}) %copy-start.5) | copy-done | bytes 2097176
  21.6 1.6 %fusion.39 = f32[8,4,128,128]{3,2,1,0:T(8,128)} fusion(f32[8,4,128,128]{3,2,1,0:T(8,128)S(1)} %copy-done.5), kind=kOutput, calls=%fused_computation.62 | output fusion | flops 1572864 | bytes 4194304 | tf_op jit(solution)/shard_map/jit(cumsum)/reduce_window_sum | solution.py:61
  23.7 7.5 %fusion.40 = f32[8,4,128,128]{3,2,1,0:T(8,128)} fusion(f32[8,4,128,128]{3,2,1,0:T(8,128)S(1)} %bitcast.87, f32[8,4,128,128]{3,2,1,0:T(8,128)} %bitcast.94), kind=kOutput, calls=%fused_computation.63 | convolution fusion | flops 805306368 | bytes 6291456 | tf_op jit(solution)/shard_map/hnqd,hnkd->hnqk/dot_general | solution.py:64
  31.2 1.8 %collective-permute-start.3 = (f32[8,128,128]{2,1,0:T(8,128)S(1)}, f32[8,128,128]{2,1,0:T(8,128)}, u32[]{:S(2)}, u32[]{:S(2)}) collective-permute-start(f32[8,128,128]{2,1,0:T(8,128)S(1)} %add.75), channel_id=1, source_target_pairs={{0,16},{16,0},{8,24},{24,8},{32,48},{48,32},{40,56},{56,40},{64,80... | collective-permute-start | bytes 1572872 | tf_op jit(solution)/shard_map/ppermute | solution.py:26
  33.0 4.6 %fusion.18 = f32[8,4,128,128]{3,2,1,0:T(8,128)S(1)} fusion(f32[8,4,128,128]{3,2,1,0:T(8,128)} %bitcast.92, f32[8,4,128,128]{3,2,1,0:T(8,128)} %fusion.40, pred[128,128]{1,0:T(8,128)(4,1)S(1)} %iota_compare_fusion), kind=kOutput, calls=%fused_computation.31 | convolution fusion | flops 805830656 | bytes 6307840 | tf_op jit(solution)/shard_map/hnqk,hnke->hnqe/dot_general | solution.py:66
  37.6 8.3 %collective-permute-done.3 = f32[8,128,128]{2,1,0:T(8,128)} collective-permute-done((f32[8,128,128]{2,1,0:T(8,128)S(1)}, f32[8,128,128]{2,1,0:T(8,128)}, u32[]{:S(2)}, u32[]{:S(2)}) %collective-permute-start.3) | collective-permute-done | bytes 524320 | tf_op jit(solution)/shard_map/ppermute | solution.py:26
  45.9 1.1 add.78
  47.0 2.8 %collective-permute-start.4 = (f32[8,128,128]{2,1,0:T(8,128)S(1)}, f32[8,128,128]{2,1,0:T(8,128)S(1)}, u32[]{:S(2)}, u32[]{:S(2)}) collective-permute-start(f32[8,128,128]{2,1,0:T(8,128)S(1)} %add.78), channel_id=1, source_target_pairs={{0,32},{32,0},{8,40},{40,8},{16,48},{48,16},{24,56},{56,24},{64,96... | collective-permute-start | bytes 1572872 | tf_op jit(solution)/shard_map/ppermute | solution.py:26
  49.8 1.2 %bitcast_bitcast_fusion.1 = f32[8,640,128]{2,1,0:T(8,128)S(1)} fusion(f32[512,1024]{1,0:T(8,128)S(1)} %copy-done.1, f32[128,1024]{1,0:T(8,128)} %collective-permute-done), kind=kLoop, calls=%fused_computation.13 | loop fusion | flops 655360 | bytes 5242880 | tf_op jit(solution)/shard_map/transpose | solution.py:41
  51.2 1.4 %copy-done.4 = f32[512,8,128]{2,0,1:T(8,128)S(1)} copy-done((f32[512,8,128]{2,0,1:T(8,128)S(1)}, f32[512,8,128]{2,0,1:T(8,128)}, u32[]{:S(2)}) %copy-start.4) | copy-done | bytes 2097176
  52.6 5.0 %fusion.9 = (f32[8,4,128]{2,1,0:T(4,128)S(1)}, f32[8,4,256,128]{3,2,1,0:T(8,128)S(1)}) fusion(pred[4,128,256]{1,2,0:T(8,128)(4,1)S(1)} %broadcast_and_fusion, f32[8,4,128,128]{3,2,1,0:T(8,128)S(1)} %bitcast.88, f32[8,4,128,128]{3,2,1,0:T(8,128)S(1)} %bitcast.95, f32[8,4,128,128]{3,2,1,0:T(8,128)S(1)} %bitcast.99), kind=kOutput, calls=%fused_computation.11 | convolution fusion | flops 1614802944 | bytes 10633216 | tf_op jit(solution)/shard_map/hnqd,hnkd->hnqk/dot_general | solution.py:81
  57.7 4.4 %collective-permute-done.4 = f32[8,128,128]{2,1,0:T(8,128)S(1)} collective-permute-done((f32[8,128,128]{2,1,0:T(8,128)S(1)}, f32[8,128,128]{2,1,0:T(8,128)S(1)}, u32[]{:S(2)}, u32[]{:S(2)}) %collective-permute-start.4) | collective-permute-done | bytes 524320 | tf_op jit(solution)/shard_map/ppermute | solution.py:26
  62.2 1.2 %bitcast_bitcast_fusion = f32[8,640,128]{2,1,0:T(8,128)S(1)} fusion(f32[512,1024]{1,0:T(8,128)S(1)} %copy-done.7, f32[128,1024]{1,0:T(8,128)} %collective-permute-done.1), kind=kLoop, calls=%fused_computation.12 | loop fusion | flops 655360 | bytes 5242880 | tf_op jit(solution)/shard_map/transpose | solution.py:41
  63.4 1.5 %copy-done.8 = f32[8,640,128]{2,1,0:T(8,128)} copy-done((f32[8,640,128]{2,1,0:T(8,128)}, f32[8,640,128]{2,1,0:T(8,128)S(1)}, u32[]{:S(2)}) %copy-start.8) | copy-done | bytes 2621464
  64.9 1.0 fusion.8
  65.9 8.8 %collective-permute-done.5 = f32[8,128,128]{2,1,0:T(8,128)S(1)} collective-permute-done((f32[8,128,128]{2,1,0:T(8,128)S(1)}, f32[8,128,128]{2,1,0:T(8,128)S(1)}, u32[]{:S(2)}, u32[]{:S(2)}) %collective-permute-start.5) | collective-permute-done | bytes 524320 | tf_op jit(solution)/shard_map/ppermute | solution.py:26
  74.8 2.6 %collective-permute-start.6 = (f32[8,128,128]{2,1,0:T(8,128)S(1)}, f32[8,128,128]{2,1,0:T(8,128)S(1)}, u32[]{:S(2)}, u32[]{:S(2)}) collective-permute-start(f32[8,128,128]{2,1,0:T(8,128)S(1)} %add.84), channel_id=1, source_target_pairs={{0,128},{128,0},{8,136},{136,8},{16,144},{144,16},{24,152},{152,24... | collective-permute-start | bytes 1572872 | tf_op jit(solution)/shard_map/ppermute | solution.py:26
  77.4 9.4 %multiply_reduce_fusion.1 = (f32[4,128]{1,0:T(4,128)S(1)}, f32[8,4,128,128]{3,2,1,0:T(8,128)}) fusion(f32[8]{0:T(128)S(1)} %get-tuple-element.7, f32[8,4,128]{2,1,0:T(4,128)S(1)} %fusion.8, f32[8,4,128,128]{3,2,1,0:T(8,128)S(1)} %bitcast.93, f32[8,4,128,128]{3,2,1,0:T(8,128)S(1)} %bitcast.96, f32[8,4,256,128]{3,2,1,0:T(8,128)S(1)} %get-tuple-element.12, ...), kind=kOutput, calls=%fused_computation.33 | convolution fusion | flops 1616903680 | bytes 10651680 | tf_op jit(solution)/shard_map/hnqk,hnkd->hnqd/dot_general | solution.py:92
  86.8 1.6 %collective-permute-done.6 = f32[8,128,128]{2,1,0:T(8,128)S(1)} collective-permute-done((f32[8,128,128]{2,1,0:T(8,128)S(1)}, f32[8,128,128]{2,1,0:T(8,128)S(1)}, u32[]{:S(2)}, u32[]{:S(2)}) %collective-permute-start.6) | collective-permute-done | bytes 524320 | tf_op jit(solution)/shard_map/ppermute | solution.py:26
  88.6 3.9 %multiply_reduce_fusion = (f32[4,128]{1,0:T(4,128)S(1)}, f32[8,4,128,128]{3,2,1,0:T(8,128)}) fusion(f32[8]{0:T(128)S(1)} %get-tuple-element.8, f32[8,4,128,128]{3,2,1,0:T(8,128)S(1)} %fusion.18, f32[8,4,128,128]{3,2,1,0:T(8,128)S(1)} %bitcast.89, f32[8,4,128,128]{3,2,1,0:T(8,128)S(1)} %copy-done.9, f32[8,4,128,128]{3,2,1,0:T(8,128)S(1)} %copy-done.6, ...), kind=kOutput, calls=%fused_computation.27 | convolution fusion | flops 808451584 | bytes 11012128 | tf_op jit(solution)/shard_map/hnqd,hnde->hnqe/dot_general | solution.py:67
  92.5 19.9 %all-reduce = (f32[512]{0:T(512)S(1)}, f32[512]{0:T(512)S(1)}) all-reduce(f32[512]{0:T(512)S(1)} %bitcast.101, f32[512]{0:T(512)S(1)} %bitcast.102), channel_id=1, replica_groups=mesh['ctx'=32,'head'=8] {'head'}, use_global_device_ids=true, to_apply=%region_7.8 | all-reduce | flops 1024 | bytes 8192 | tf_op jit(solution)/shard_map/psum | solution.py:100
  112.4 2.7 %fusion.11 = f32[8,512,128]{2,1,0:T(8,128)S(1)} fusion(f32[8,4,128,128]{3,2,1,0:T(8,128)} %get-tuple-element.14, f32[8,4,128,128]{3,2,1,0:T(8,128)} %get-tuple-element.16, f32[512]{0:T(512)S(1)} %get-tuple-element.17, f32[8]{0:T(128)S(1)} %get-tuple-element.8, f32[512]{0:T(512)S(1)} %get-tuple-element.18, f32[8]{0:T(128)S(1)} %get-tuple-element.7), kind=kLoop, calls=%fused_computation.21 | loop fusion | flops 2621440 | bytes 6295616 | tf_op jit(solution)/shard_map/add | solution.py:103
  115.1 1.6 %copy_bitcast_fusion = f32[512,1024]{1,0:T(8,128)} fusion(f32[8,512,128]{2,1,0:T(8,128)S(1)} %fusion.11), kind=kLoop, calls=%fused_computation.16 | loop fusion | bytes 4194304 | tf_op jit(solution)/shard_map/reshape | solution.py:104
  (45 shorter events, 2.3 us)
Async XLA Ops:
  0.0 2.2 %copy-start = (f32[512,1024]{1,0:T(8,128)S(1)}, f32[512,1024]{1,0:T(8,128)}, u32[]{:S(2)}) copy-start(f32[512,1024]{1,0:T(8,128)} %param.5) | copy-start | bytes 6291460
  1.9 1.3 %copy-start.2 = (f32[512,8,128]{2,0,1:T(8,128)}, f32[512,8,128]{2,0,1:T(8,128)S(1)}, u32[]{:S(2)}) copy-start(f32[512,8,128]{2,0,1:T(8,128)S(1)} %copy_bitcast_fusion.1) | copy-start | bytes 6291460
  8.3 9.7 %copy-start.10 = (f32[8,128,128]{2,1,0:T(8,128)}, f32[8,128,128]{2,1,0:T(8,128)S(1)}, u32[]{:S(2)}) copy-start(f32[8,128,128]{2,1,0:T(8,128)S(1)} %get-tuple-element.9) | copy-start | bytes 1572868
  8.3 22.9 %collective-permute-start.2 = (f32[8,128,128]{2,1,0:T(8,128)S(1)}, f32[8,128,128]{2,1,0:T(8,128)S(1)}, u32[]{:S(2)}, u32[]{:S(2)}) collective-permute-start(f32[8,128,128]{2,1,0:T(8,128)S(1)} %get-tuple-element.9), channel_id=1, source_target_pairs={{0,8},{8,0},{16,24},{24,16},{32,40},{40,32},{48,56},{56,48},{64,72... | collective-permute-start | bytes 1572872 | tf_op jit(solution)/shard_map/ppermute | solution.py:26
  9.2 40.6 %collective-permute-start = (f32[128,1024]{1,0:T(8,128)}, f32[128,1024]{1,0:T(8,128)}, u32[]{:S(2)}, u32[]{:S(2)}) collective-permute-start(f32[128,1024]{1,0:T(8,128)} %slice.18), channel_id=1, source_target_pairs={{0,8},{8,16},{16,24},{24,32},{32,40},{40,48},{48,56},{56,64},{64,7... | collective-permute-start | bytes 1572872 | tf_op jit(solution)/shard_map/ppermute | solution.py:16
  13.4 48.8 %collective-permute-start.1 = (f32[128,1024]{1,0:T(8,128)}, f32[128,1024]{1,0:T(8,128)}, u32[]{:S(2)}, u32[]{:S(2)}) collective-permute-start(f32[128,1024]{1,0:T(8,128)} %slice.20), channel_id=1, source_target_pairs={{0,8},{8,16},{16,24},{24,32},{32,40},{40,48},{48,56},{56,64},{64,7... | collective-permute-start | bytes 1572872 | tf_op jit(solution)/shard_map/ppermute | solution.py:16
  20.1 1.6 %copy-start.5 = (f32[8,4,128,128]{3,2,1,0:T(8,128)S(1)}, f32[8,4,128,128]{3,2,1,0:T(8,128)}, u32[]{:S(2)}) copy-start(f32[8,4,128,128]{3,2,1,0:T(8,128)} %get-tuple-element.10) | copy-start | bytes 6291460
  23.6 7.5 %copy-start.11 = (f32[8,128,128]{2,1,0:T(8,128)S(1)}, f32[8,128,128]{2,1,0:T(8,128)}, u32[]{:S(2)}) copy-start(f32[8,128,128]{2,1,0:T(8,128)} %copy-done.10) | copy-start | bytes 1572868
  23.6 9.4 %copy-start.12 = (f32[2,8]{1,0:T(2,128)S(1)}, f32[2,8]{1,0:T(2,128)}, u32[]{:S(2)}) copy-start(f32[2,8]{1,0:T(2,128)} %param.7) | copy-start | bytes 196
  31.2 14.7 %collective-permute-start.3 = (f32[8,128,128]{2,1,0:T(8,128)S(1)}, f32[8,128,128]{2,1,0:T(8,128)}, u32[]{:S(2)}, u32[]{:S(2)}) collective-permute-start(f32[8,128,128]{2,1,0:T(8,128)S(1)} %add.75), channel_id=1, source_target_pairs={{0,16},{16,0},{8,24},{24,8},{32,48},{48,32},{40,56},{56,40},{64,80... | collective-permute-start | bytes 1572872 | tf_op jit(solution)/shard_map/ppermute | solution.py:26
  33.0 16.8 %copy-start.1 = (f32[512,1024]{1,0:T(8,128)S(1)}, f32[512,1024]{1,0:T(8,128)}, u32[]{:S(2)}) copy-start(f32[512,1024]{1,0:T(8,128)} %param.5) | copy-start | bytes 6291460
  47.0 15.0 %collective-permute-start.4 = (f32[8,128,128]{2,1,0:T(8,128)S(1)}, f32[8,128,128]{2,1,0:T(8,128)S(1)}, u32[]{:S(2)}, u32[]{:S(2)}) collective-permute-start(f32[8,128,128]{2,1,0:T(8,128)S(1)} %add.78), channel_id=1, source_target_pairs={{0,32},{32,0},{8,40},{40,8},{16,48},{48,16},{24,56},{56,24},{64,96... | collective-permute-start | bytes 1572872 | tf_op jit(solution)/shard_map/ppermute | solution.py:26
  51.0 1.6 %copy-start.4 = (f32[512,8,128]{2,0,1:T(8,128)S(1)}, f32[512,8,128]{2,0,1:T(8,128)}, u32[]{:S(2)}) copy-start(f32[512,8,128]{2,0,1:T(8,128)} %copy_bitcast_fusion.2) | copy-start | bytes 6291460
  52.6 9.6 %copy-start.7 = (f32[512,1024]{1,0:T(8,128)S(1)}, f32[512,1024]{1,0:T(8,128)}, u32[]{:S(2)}) copy-start(f32[512,1024]{1,0:T(8,128)} %param.6) | copy-start | bytes 6291460
  62.1 12.7 %collective-permute-start.5 = (f32[8,128,128]{2,1,0:T(8,128)S(1)}, f32[8,128,128]{2,1,0:T(8,128)S(1)}, u32[]{:S(2)}, u32[]{:S(2)}) collective-permute-start(f32[8,128,128]{2,1,0:T(8,128)S(1)} %add.81), channel_id=1, source_target_pairs={{0,64},{64,0},{8,72},{72,8},{16,80},{80,16},{24,88},{88,24},{32,96... | collective-permute-start | bytes 1572872 | tf_op jit(solution)/shard_map/ppermute | solution.py:26
  63.4 1.5 %copy-start.8 = (f32[8,640,128]{2,1,0:T(8,128)}, f32[8,640,128]{2,1,0:T(8,128)S(1)}, u32[]{:S(2)}) copy-start(f32[8,640,128]{2,1,0:T(8,128)S(1)} %bitcast_bitcast_fusion) | copy-start | bytes 7864324
  64.9 12.5 %copy-start.3 = (f32[512,8,128]{2,0,1:T(8,128)S(1)}, f32[512,8,128]{2,0,1:T(8,128)}, u32[]{:S(2)}) copy-start(f32[512,8,128]{2,0,1:T(8,128)} %copy-done.2) | copy-start | bytes 6291460
  64.9 12.5 %slice-start = ((f32[8,640,128]{2,1,0:T(8,128)}), f32[8,512,128]{2,1,0:T(8,128)S(1)}, s32[]{:S(2)}) async-start(f32[8,640,128]{2,1,0:T(8,128)} %copy-done.8), calls=%async_computation | async-start | bytes 4194304 | tf_op jit(solution)/shard_map/slice | solution.py:78
  74.8 13.5 %collective-permute-start.6 = (f32[8,128,128]{2,1,0:T(8,128)S(1)}, f32[8,128,128]{2,1,0:T(8,128)S(1)}, u32[]{:S(2)}, u32[]{:S(2)}) collective-permute-start(f32[8,128,128]{2,1,0:T(8,128)S(1)} %add.84), channel_id=1, source_target_pairs={{0,128},{128,0},{8,136},{136,8},{16,144},{144,16},{24,152},{152,24... | collective-permute-start | bytes 1572872 | tf_op jit(solution)/shard_map/ppermute | solution.py:26
  77.4 11.2 %copy-start.9 = (f32[8,4,128,128]{3,2,1,0:T(8,128)S(1)}, f32[8,4,128,128]{3,2,1,0:T(8,128)}, u32[]{:S(2)}) copy-start(f32[8,4,128,128]{3,2,1,0:T(8,128)} %fusion.39) | copy-start | bytes 6291460
  86.8 1.8 %copy-start.6 = (f32[8,4,128,128]{3,2,1,0:T(8,128)S(1)}, f32[8,4,128,128]{3,2,1,0:T(8,128)}, u32[]{:S(2)}) copy-start(f32[8,4,128,128]{3,2,1,0:T(8,128)} %get-tuple-element.10) | copy-start | bytes 6291460
where the time goes:
time: 118 us; the launch traced here: 117 us
  matrix products  35.4 us (30%)
  waiting for transfers between devices  23.1 us (20%)
  blocking collectives  19.9 us (17%)
  local copies, waits for them, and re-layouts  15.8 us (13%)
  starting transfers between devices  12.6 us (11%)
  other arithmetic  9.57 us (8%)
    ppermute x5, waiting for transfers between devices, swapped(): return lax.ppermute(block, axis, route)  23.1 us
    psum x1, blocking collectives, shards(): square_a, square_b = lax.psum((square_a, square_b), 'head')  19.9 us
    dot_general x1, matrix products, shards(): jnp.einsum('hnqk,hnkd->hnqd', weights, value_both, precision=highest)  9.35 us
    unnamed x28, local copies, waits for them, and re-layouts  7.51 us
    dot_general x1, matrix products, shards(): jnp.einsum('hnqd,hnkd->hnqk', query_blocks, key_blocks, precision=highest)  7.5 us
    ppermute x5, starting transfers between devices, swapped(): return lax.ppermute(block, axis, route)  7.24 us
    ppermute x2, starting transfers between devices, shifted(): return lax.ppermute(block, axis, route)  5.4 us
    dot_general x1, matrix products, shards(): jnp.einsum('hnkd,hnke->hnde', key_blocks, value_blocks, precision=highest)  5.07 us
  transfers between devices with their start and end apart: 7, of which 4 were waited for; matrix products, arithmetic and copies ran while one was open for 34% of the time, Pallas kernels for 0%

commit v1 on v0

v1 whole, which is shorter than its diff:
```python
import functools
import math

import jax
import jax.numpy as jnp
from jax import lax
from jax.experimental import pallas as pl
from jax.experimental.pallas import tpu as pltpu
from jax.sharding import PartitionSpec as P

HEADS = 64
HD = 128
WINDOW = 128
MESH = pl.DeviceIdType.MESH
F32 = jnp.float32
BF16 = jnp.bfloat16


def split(x):
    high = x.astype(BF16)
    low = (x - high.astype(F32)).astype(BF16)
    return high, low


def dot(a, b, ca, cb):
    return lax.dot_general(a, b, (((ca,), (cb,)), ((), ())), preferred_element_type=F32)


def wide(x):
    both = jnp.concatenate(split(x), axis=1)
    return jnp.concatenate([both, both], axis=0)


def kernel(
    ctx_count, head_axis, heads, rows,
    q_hbm, k_hbm, v_hbm, gain,
    out,
    kbuf, vbuf, qbuf, halo, k2, v2, q2, first, total, pair, chip, gather, prefix, piece_in, state, cross,
    a_buf, b_buf, acc_a, acc_b, zsend, zbuf,
    load_sem, halo_send, halo_recv, pair_send, pair_recv, gather_send, gather_recv,
    prefix_send, prefix_recv, cross_send, cross_recv, z_send, z_recv,
):
    ctx = lax.axis_index("ctx")
    z = lax.axis_index("head")
    core = lax.rem(ctx, 2)
    mine = lax.div(ctx, 2)
    chips = ctx_count // 2
    half = heads // 2
    per_head = chips // half
    depth = HD // per_head
    blocks = rows // HD
    factor = 1.0 / math.sqrt(HD)
    sibling = (ctx + 1 - 2 * core, z)
    following = (lax.rem(ctx + 1, ctx_count), z)
    preceding = (lax.rem(ctx + ctx_count - 1, ctx_count), z)
    side = 4 if chips == 16 else 0

    def owner(j, i):
        if side:
            return side * i + lax.rem(i + j, side)
        return j * per_head + i

    def piece_of(c):
        if side:
            y = lax.div(c, side)
            x = lax.rem(c, side)
            return side * lax.rem(x + side - y, side) + y
        return c

    def load(source, target, slot, h):
        columns = pl.ds(pl.multiple_of(h * HD, HD), HD)
        return pltpu.make_async_copy(source.at[:, columns], target.at[h], load_sem.at[slot, h])

    barrier = pltpu.get_barrier_semaphore()

    def greet(device):
        pl.semaphore_signal(barrier, inc=1, device_id=device, device_id_type=MESH)

    for jj in range(heads):
        h = lax.rem(jj + half * (1 - core), heads)
        load(k_hbm, kbuf, 0, h).start()
        load(v_hbm, vbuf, 1, h).start()
    greet(following)
    greet(preceding)
    greet(sibling)
    for d in range(1, chips):
        greet((2 * lax.rem(mine + d, chips) + core, z))
    for d in range(1, head_axis):
        greet((ctx, lax.rem(z + d, head_axis)))
    for h in range(heads):
        load(q_hbm, qbuf, 2, h).start()
    pl.semaphore_wait(barrier, 3 + chips - 1 + head_axis - 1)

    def halo_copy(slot):
        return pltpu.make_async_remote_copy(
            src_ref=(k_hbm, v_hbm)[slot].at[pl.ds(rows - HD, HD), :],
            dst_ref=halo.at[slot],
            send_sem=halo_send.at[slot],
            recv_sem=halo_recv.at[slot],
            device_id=following,
            device_id_type=MESH,
        )

    halo_copy(0).start()
    halo_copy(1).start()

    def local_state(h):
        load(k_hbm, kbuf, 0, h).wait()
        load(v_hbm, vbuf, 1, h).wait()
        k_high, k_low = split(kbuf[h])
        v_high, v_low = split(vbuf[h])
        k2[h, HD:, :HD] = k_high
        k2[h, HD:, HD:] = k_low
        v2[h, HD:, :HD] = v_high
        v2[h, HD:, HD:] = v_low
        kk = jnp.concatenate([k_high, k_low], axis=1)
        vv = jnp.concatenate([v_high, v_low], axis=1)
        mid = rows // 2
        parts = []
        for part in range(2):
            r = dot(kk[part * mid : (part + 1) * mid], vv[part * mid : (part + 1) * mid], 0, 0)
            parts.append(r[:HD, :HD] + (r[:HD, HD:] + r[HD:, :HD]))
        first[h] = parts[0]
        total[h] = parts[0] + parts[1]

    def pair_copy(j):
        return pltpu.make_async_remote_copy(
            src_ref=total.at[half * (1 - core) + j],
            dst_ref=pair.at[j],
            send_sem=pair_send.at[j],
            recv_sem=pair_recv.at[j],
            device_id=sibling,
            device_id_type=MESH,
        )

    def gather_copy(j, i, target, slot):
        return pltpu.make_async_remote_copy(
            src_ref=chip.at[j, pl.ds(i * depth, depth), :],
            dst_ref=gather.at[slot],
            send_sem=gather_send.at[j, i],
            recv_sem=gather_recv.at[slot],
            device_id=(2 * target + core, z),
            device_id_type=MESH,
        )

    @pl.loop(0, half)
    def _(j):
        local_state(half * (1 - core) + j)
        pair_copy(j).start()

    @pl.loop(0, half)
    def _(j):
        h = half * core + j
        local_state(h)
        pair_copy(j).wait_recv()
        chip[j] = total[h] + pair[j]
        for i in range(per_head):
            target = owner(j, i)

            @pl.when(target == mine)
            def _():
                gather[mine] = chip[j, i * depth : (i + 1) * depth, :]

            @pl.when(target != mine)
            def _():
                gather_copy(j, i, target, mine).start()

    row = lax.broadcasted_iota(jnp.int32, (HD, 2 * HD), 0)
    col = lax.broadcasted_iota(jnp.int32, (HD, 2 * HD), 1)
    band = (col > row) & (col <= row + HD)
    causal_even = (col >= HD) & (col <= row + HD)
    causal_odd = col <= row + HD

    acc_a[...] = jnp.zeros_like(acc_a)
    acc_b[...] = jnp.zeros_like(acc_b)

    def block(h, n, allowed, causal):
        here = slice(n * HD, (n + 1) * HD)
        both = slice(n * HD, (n + 2) * HD)
        q_low_high = q2[h, here, :]
        k_pair = k2[h, both, :]
        s = dot(q_low_high[:, HD:], k_pair[:, :HD], 1, 1) + dot(q_low_high, k_pair, 1, 1)
        masked = jnp.where(allowed, s, -jnp.inf)
        biggest = jnp.max(masked, axis=1, keepdims=True)
        weights = jnp.exp((masked - biggest) * factor)
        weight_sum = jnp.sum(weights, axis=1, keepdims=True)
        inner = jnp.where(causal, s, 0.0)
        stacked = jnp.concatenate(split(weights) + split(inner), axis=0)
        r = dot(stacked, v2[h, both, :], 1, 0)
        win = r[:HD, :HD] + (r[:HD, HD:] + r[HD : 2 * HD, :HD])
        lin = r[2 * HD : 3 * HD, :HD] + (r[2 * HD : 3 * HD, HD:] + r[3 * HD :, :HD])
        a = win * (gain[0, h] / weight_sum)
        a_buf[h, here, :] = a
        acc_a[here, :] += a * a
        return lin

    def inner_blocks(h):
        load(q_hbm, qbuf, 2, h).wait()
        q_high, q_low = split(qbuf[h])
        q2[h, :, :HD] = q_low
        q2[h, :, HD:] = q_high
        mid = rows // 2
        carried = dot(q2[h, mid:, :], wide(first[h]), 1, 0)
        carried = carried[:, :HD] + carried[:, HD:]
        for n in range(1, blocks):
            lin = block(h, n, band, causal_odd if n % 2 else causal_even)
            if n * HD >= mid:
                lin = lin + carried[n * HD - mid : (n + 1) * HD - mid]
            b_buf[h, n * HD : (n + 1) * HD, :] = lin

    cut = heads // 2

    @pl.loop(0, cut)
    def _(h):
        inner_blocks(h)

    def prefix_copy(d, slot):
        target = lax.rem(mine + d, chips)
        return pltpu.make_async_remote_copy(
            src_ref=prefix.at[target],
            dst_ref=piece_in.at[slot],
            send_sem=prefix_send.at[d],
            recv_sem=prefix_recv.at[slot],
            device_id=(2 * target + core, z),
            device_id_type=MESH,
        )

    @pl.loop(1, chips)
    def _(d):
        gather_copy(0, 0, mine, lax.rem(mine + d, chips)).wait_recv()

    running = jnp.zeros((depth, HD), F32)
    for c in range(chips):
        prefix[c] = running
        if c < chips - 1:
            running = running + gather[c]
    my_piece = piece_of(mine)
    piece_in[my_piece] = prefix[mine]

    @pl.loop(1, chips)
    def _(d):
        prefix_copy(d, my_piece).start()

    @pl.loop(cut, heads)
    def _(h):
        inner_blocks(h)

    def cross_copy(j):
        return pltpu.make_async_remote_copy(
            src_ref=cross.at[j],
            dst_ref=state.at[half * core + j],
            send_sem=cross_send.at[j],
            recv_sem=cross_recv.at[j],
            device_id=sibling,
            device_id_type=MESH,
        )

    @pl.loop(0, half)
    def _(j):
        h = half * core + j
        for i in range(per_head):
            p = j * per_head + i

            @pl.when(p != my_piece)
            def _():
                prefix_copy(1, p).wait_recv()

        before = piece_in[pl.ds(j * per_head, per_head)].reshape(HD, HD)
        state[h] = before + jnp.where(core == 1, pair[j], 0.0)
        cross[j] = before + jnp.where(core == 0, total[h], 0.0)
        cross_copy(j).start()

    halo_copy(0).wait_recv()
    halo_copy(1).wait_recv()
    band_first = band & ((col >= HD) | (ctx > 0))

    @pl.loop(0, heads)
    def _(h):
        columns = pl.ds(pl.multiple_of(h * HD, HD), HD)
        k_high, k_low = split(halo[0, :, columns])
        v_high, v_low = split(halo[1, :, columns])
        k2[h, :HD, :HD] = k_high
        k2[h, :HD, HD:] = k_low
        v2[h, :HD, :HD] = v_high
        v2[h, :HD, HD:] = v_low
        b_buf[h, :HD, :] = block(h, 0, band_first, causal_even)

    def last_linear(h):
        r = dot(q2[h], wide(state[h]), 1, 0)
        b = (b_buf[h] + (r[:, :HD] + r[:, HD:])) * gain[1, h]
        b_buf[h] = b
        acc_b[...] += b * b

    @pl.loop(0, half)
    def _(j):
        last_linear(half * core + j)

    @pl.loop(0, half)
    def _(j):
        cross_copy(j).wait_recv()
        last_linear(half * (1 - core) + j)

    sums = []
    for acc in (acc_a, acc_b):
        for n in range(blocks):
            turned = jnp.transpose(acc[n * HD : (n + 1) * HD, :])
            sums.append(jnp.sum(turned, axis=0, keepdims=True))
    sums = jnp.concatenate(sums, axis=0)
    zsend[...] = sums
    zbuf[z] = sums

    def z_copy(d, slot):
        return pltpu.make_async_remote_copy(
            src_ref=zsend,
            dst_ref=zbuf.at[slot],
            send_sem=z_send.at[d],
            recv_sem=z_recv.at[slot],
            device_id=(ctx, lax.rem(z + d, head_axis)),
            device_id_type=MESH,
        )

    for d in range(1, head_axis):
        z_copy(d, z).start()
    for d in range(1, head_axis):
        z_copy(d, lax.rem(z + d, head_axis)).wait_recv()
    squares = zbuf[0]
    for other in range(1, head_axis):
        squares = squares + zbuf[other]
    inverse = 1.0 / jnp.sqrt(squares / (heads * head_axis * HD) + 1e-06)
    inverse = jnp.concatenate([inverse, jnp.zeros((HD - 2 * blocks, HD), F32)], axis=0)
    columns = jnp.transpose(inverse)
    for n in range(blocks):
        here = slice(n * HD, (n + 1) * HD)
        scale_a = columns[:, n : n + 1]
        scale_b = columns[:, blocks + n : blocks + n + 1]
        for h in range(heads):
            out[here, h * HD : (h + 1) * HD] = a_buf[h, here, :] * scale_a + b_buf[h, here, :] * scale_b

    for slot in range(2):
        halo_copy(slot).wait_send()
    for d in range(1, head_axis):
        z_copy(d, z).wait_send()

    @pl.loop(0, half)
    def _(j):
        pair_copy(j).wait_send()
        cross_copy(j).wait_send()
        for i in range(per_head):
            @pl.when(owner(j, i) != mine)
            def _():
                gather_copy(j, i, owner(j, i), mine).wait_send()

    @pl.loop(1, chips)
    def _(d):
        prefix_copy(d, my_piece).wait_send()


def shards(ctx_count, head_axis, queries, keys, values, head_gain):
    rows = queries.shape[0]
    heads = head_gain.shape[1]
    chips = ctx_count // 2
    half = heads // 2
    depth = half * HD // chips
    per_head = chips // half
    blocks = rows // HD
    anywhere = pl.BlockSpec(memory_space=pl.ANY)
    dma = pltpu.SemaphoreType.DMA
    vmem = pltpu.VMEM
    body = functools.partial(kernel, ctx_count, head_axis, heads, rows)
    return pl.pallas_call(
        body,
        out_shape=jax.ShapeDtypeStruct((rows, heads * HD), F32),
        in_specs=[anywhere, anywhere, anywhere, pl.BlockSpec(memory_space=pltpu.SMEM)],
        out_specs=pl.BlockSpec(memory_space=pltpu.VMEM),
        scratch_shapes=[
            vmem((heads, rows, HD), F32),
            vmem((heads, rows, HD), F32),
            vmem((heads, rows, HD), F32),
            vmem((2, HD, heads * HD), F32),
            vmem((heads, rows + HD, 2 * HD), BF16),
            vmem((heads, rows + HD, 2 * HD), BF16),
            vmem((heads, rows, 2 * HD), BF16),
            vmem((heads, HD, HD), F32),
            vmem((heads, HD, HD), F32),
            vmem((half, HD, HD), F32),
            vmem((half, HD, HD), F32),
            vmem((chips, depth, HD), F32),
            vmem((chips, depth, HD), F32),
            vmem((chips, depth, HD), F32),
            vmem((heads, HD, HD), F32),
            vmem((half, HD, HD), F32),
            vmem((heads, rows, HD), F32),
            vmem((heads, rows, HD), F32),
            vmem((rows, HD), F32),
            vmem((rows, HD), F32),
            vmem((2 * blocks, HD), F32),
            vmem((head_axis, 2 * blocks, HD), F32),
            dma((3, heads)),
            dma((2,)),
            dma((2,)),
            dma((half,)),
            dma((half,)),
            dma((half, per_head)),
            dma((chips,)),
            dma((chips,)),
            dma((chips,)),
            dma((half,)),
            dma((half,)),
            dma((head_axis,)),
            dma((head_axis,)),
        ],
        compiler_params=pltpu.CompilerParams(
            collective_id=0, has_side_effects=True, vmem_limit_bytes=60 * 1024 * 1024
        ),
    )(queries, keys, values, head_gain)


def solution(mesh):
    body = functools.partial(shards, mesh.shape["ctx"], mesh.shape["head"])
    in_specs = (P("ctx", "head"), P("ctx", "head"), P("ctx", "head"), P(None, "head"))
    return jax.shard_map(body, mesh=mesh, in_specs=in_specs, out_specs=P("ctx", "head"), check_vma=False)
```

time: 118 us -> 50.6 us (0.43)
  the two profiles are of different devices: /device:TPU:8 before, /device:TPU:1 now
where the time goes in v1:
time: 50.6 us; the launch traced here: 50.5 us
  Pallas kernels  47.3 us (93%)
  local copies, waits for them, and re-layouts  3.16 us (6%)
    pallas_call x1, Pallas kernels, shards(): pl.pallas_call(body, out_shape=jax.ShapeDtypeStruct((rows, heads * HD), F...  47.3 us
    unnamed x1, local copies, waits for them, and re-layouts  3.16 us

profile of v1, /device:TPU:1, one launch (start us, length us, event | category | flops | bytes accessed | tf_op | source)
XLA Modules:
  0.0 50.5 jit_solution(5752607445110819530)
XLA Ops:
  0.0 47.3 %shard_map.46 = f32[512,1024]{1,0:T(8,128)} custom-call(f32[512,1024]{1,0:T(8,128)} %q_hbm.1, f32[512,1024]{1,0:T(8,128)} %k_hbm.1, f32[512,1024]{1,0:T(8,128)} %v_hbm.1, f32[2,8]{1,0:T(2,128)} %gain.1), custom_call_target="tpu_custom_call" | custom-call | tf_op jit(solution)/shard_map/pallas_call | solution.py:370
  47.3 3.2 %copy.6 = f32[512,1024]{1,0:T(8,128)} copy(f32[512,1024]{1,0:T(8,128)} %shard_map.46) | data formatting | bytes 4194304

commit v2 on v1

--- a/solution.py
+++ b/solution.py
@@ -35,9 +35,9 @@
     ctx_count, head_axis, heads, rows,
     q_hbm, k_hbm, v_hbm, gain,
     out,
-    kbuf, vbuf, qbuf, halo, k2, v2, q2, first, total, pair, chip, gather, prefix, piece_in, state, cross,
+    kbuf, vbuf, qbuf, asked, answer, answered, told, heard, own_peak, own_sum, k2, v2, q2, first, total, pair, chip, gather, prefix, piece_in, state, cross,
     a_buf, b_buf, acc_a, acc_b, zsend, zbuf,
-    load_sem, halo_send, halo_recv, pair_send, pair_recv, gather_send, gather_recv,
+    load_sem, ask_send, ask_recv, answer_send, answer_recv, told_send, told_recv, pair_send, pair_recv, gather_send, gather_recv,
     prefix_send, prefix_recv, cross_send, cross_recv, z_send, z_recv,
 ):
     ctx = lax.axis_index("ctx")
@@ -71,6 +71,8 @@
         columns = pl.ds(pl.multiple_of(h * HD, HD), HD)
         return pltpu.make_async_copy(source.at[:, columns], target.at[h], load_sem.at[slot, h])
 
+    sent = []
+
     barrier = pltpu.get_barrier_semaphore()
 
     def greet(device):
@@ -89,30 +91,48 @@
         greet((ctx, lax.rem(z + d, head_axis)))
     for h in range(heads):
         load(q_hbm, qbuf, 2, h).start()
-    pl.semaphore_wait(barrier, 3 + chips - 1 + head_axis - 1)
-
-    def halo_copy(slot):
-        return pltpu.make_async_remote_copy(
-            src_ref=(k_hbm, v_hbm)[slot].at[pl.ds(rows - HD, HD), :],
-            dst_ref=halo.at[slot],
-            send_sem=halo_send.at[slot],
-            recv_sem=halo_recv.at[slot],
+    groups = heads // 2
+    last = slice(rows - HD, rows)
+
+    def ask_copy(g):
+        return pltpu.make_async_remote_copy(
+            src_ref=q_hbm.at[pl.ds(0, HD), pl.ds(pl.multiple_of(g * 2 * HD, HD), 2 * HD)],
+            dst_ref=asked.at[g],
+            send_sem=ask_send.at[g],
+            recv_sem=ask_recv.at[g],
+            device_id=preceding,
+            device_id_type=MESH,
+        )
+
+    def answer_copy(g):
+        return pltpu.make_async_remote_copy(
+            src_ref=answer.at[g],
+            dst_ref=answered.at[g],
+            send_sem=answer_send.at[g],
+            recv_sem=answer_recv.at[g],
             device_id=following,
             device_id_type=MESH,
         )
 
-    halo_copy(0).start()
-    halo_copy(1).start()
+    def told_copy():
+        return pltpu.make_async_remote_copy(
+            src_ref=told,
+            dst_ref=heard,
+            send_sem=told_send,
+            recv_sem=told_recv,
+            device_id=following,
+            device_id_type=MESH,
+        )
 
     def local_state(h):
         load(k_hbm, kbuf, 0, h).wait()
         load(v_hbm, vbuf, 1, h).wait()
         k_high, k_low = split(kbuf[h])
         v_high, v_low = split(vbuf[h])
-        k2[h, HD:, :HD] = k_high
-        k2[h, HD:, HD:] = k_low
-        v2[h, HD:, :HD] = v_high
-        v2[h, HD:, HD:] = v_low
+        k2[h, :, :HD] = k_high
+        k2[h, :, HD:] = k_low
+        v2[h, :, :HD] = v_high
+        v2[h, :, HD:] = v_low
         kk = jnp.concatenate([k_high, k_low], axis=1)
         vv = jnp.concatenate([v_high, v_low], axis=1)
         mid = rows // 2
@@ -146,7 +166,20 @@
     @pl.loop(0, half)
     def _(j):
         local_state(half * (1 - core) + j)
+
+    pl.semaphore_wait(barrier, 3 + chips - 1 + head_axis - 1)
+    for j in range(half):
         pair_copy(j).start()
+    for g in range(groups):
+        ask_copy(g).start()
+        sent.append(ask_copy(g).wait_send)
+
+    def pair_done():
+        @pl.loop(0, half)
+        def _(j):
+            pair_copy(j).wait_send()
+
+    sent.append(pair_done)
 
     @pl.loop(0, half)
     def _(j):
@@ -165,21 +198,39 @@
             def _():
                 gather_copy(j, i, target, mine).start()
 
+    def gather_done():
+        @pl.loop(0, half)
+        def _(j):
+            for i in range(per_head):
+                @pl.when(owner(j, i) != mine)
+                def _():
+                    gather_copy(j, i, owner(j, i), mine).wait_send()
+
+    sent.append(gather_done)
+
     row = lax.broadcasted_iota(jnp.int32, (HD, 2 * HD), 0)
     col = lax.broadcasted_iota(jnp.int32, (HD, 2 * HD), 1)
     band = (col > row) & (col <= row + HD)
     causal_even = (col >= HD) & (col <= row + HD)
     causal_odd = col <= row + HD
+    lane = col[:, :HD]
+    lower = lane <= row[:, :HD]
 
     acc_a[...] = jnp.zeros_like(acc_a)
     acc_b[...] = jnp.zeros_like(acc_b)
-
-    def block(h, n, allowed, causal):
+    told[...] = jnp.zeros_like(told)
+    own_peak[...] = jnp.zeros_like(own_peak)
+    own_sum[...] = jnp.zeros_like(own_sum)
+
+    def scores(q_low_high, keys):
+        return dot(q_low_high[:, HD:], keys[:, :HD], 1, 1) + dot(q_low_high, keys, 1, 1)
+
+    def block(h, n):
         here = slice(n * HD, (n + 1) * HD)
-        both = slice(n * HD, (n + 2) * HD)
-        q_low_high = q2[h, here, :]
-        k_pair = k2[h, both, :]
-        s = dot(q_low_high[:, HD:], k_pair[:, :HD], 1, 1) + dot(q_low_high, k_pair, 1, 1)
+        both = slice(max(n - 1, 0) * HD, (n + 1) * HD)
+        allowed = band if n else lower
+        causal = (causal_odd if n % 2 else causal_even) if n else lower
+        s = scores(q2[h, here, :], k2[h, both, :])
         masked = jnp.where(allowed, s, -jnp.inf)
         biggest = jnp.max(masked, axis=1, keepdims=True)
         weights = jnp.exp((masked - biggest) * factor)
@@ -189,9 +240,14 @@
         r = dot(stacked, v2[h, both, :], 1, 0)
         win = r[:HD, :HD] + (r[:HD, HD:] + r[HD : 2 * HD, :HD])
         lin = r[2 * HD : 3 * HD, :HD] + (r[2 * HD : 3 * HD, HD:] + r[3 * HD :, :HD])
-        a = win * (gain[0, h] / weight_sum)
-        a_buf[h, here, :] = a
-        acc_a[here, :] += a * a
+        if n:
+            a = win * (gain[0, h] / weight_sum)
+            a_buf[h, here, :] = a
+            acc_a[here, :] += a * a
+        else:
+            a_buf[h, here, :] = win
+            own_peak[...] = jnp.where(lane == h, biggest, own_peak[...])
+            own_sum[...] = jnp.where(lane == h, weight_sum, own_sum[...])
         return lin
 
     def inner_blocks(h):
@@ -202,17 +258,49 @@
         mid = rows // 2
         carried = dot(q2[h, mid:, :], wide(first[h]), 1, 0)
         carried = carried[:, :HD] + carried[:, HD:]
-        for n in range(1, blocks):
-            lin = block(h, n, band, causal_odd if n % 2 else causal_even)
+        for n in range(blocks):
+            lin = block(h, n)
             if n * HD >= mid:
                 lin = lin + carried[n * HD - mid : (n + 1) * HD - mid]
             b_buf[h, n * HD : (n + 1) * HD, :] = lin
 
-    cut = heads // 2
-
-    @pl.loop(0, cut)
+    def answer_group(g):
+        ask_copy(g).wait_recv()
+        for e in range(2):
+            h = 2 * g + e
+            columns = slice(e * HD, (e + 1) * HD)
+            q_high, q_low = split(asked[g, :, columns])
+            s = scores(jnp.concatenate([q_low, q_high], axis=1), k2[h, last, :])
+            biggest = jnp.max(jnp.where(lower, -3e38, s), axis=1, keepdims=True)
+            weights = jnp.where(lower, 0.0, jnp.exp((s - biggest) * factor))
+            weight_sum = jnp.sum(weights, axis=1, keepdims=True)
+            r = dot(jnp.concatenate(split(weights), axis=0), v2[h, last, :], 1, 0)
+            answer[g, :, columns] = r[:HD, :HD] + (r[:HD, HD:] + r[HD:, :HD])
+            told[...] = jnp.where(
+                lane == h, biggest, jnp.where(lane == heads + h, weight_sum, told[...])
+            )
+        answer_copy(g).start()
+
+    early = heads - groups - 2
+
+    @pl.loop(0, early)
     def _(h):
         inner_blocks(h)
+
+    @pl.loop(0, groups)
+    def _(g):
+        answer_group(g)
+        inner_blocks(early + g)
+
+    def answer_done():
+        @pl.loop(0, groups)
+        def _(g):
+            answer_copy(g).wait_send()
+
+        told_copy().wait_send()
+
+    told_copy().start()
+    sent.append(answer_done)
 
     def prefix_copy(d, slot):
         target = lax.rem(mine + d, chips)
@@ -241,7 +329,14 @@
     def _(d):
         prefix_copy(d, my_piece).start()
 
-    @pl.loop(cut, heads)
+    def prefix_done():
+        @pl.loop(1, chips)
+        def _(d):
+            prefix_copy(d, my_piece).wait_send()
+
+    sent.append(prefix_done)
+
+    @pl.loop(early + groups, heads)
     def _(h):
         inner_blocks(h)
 
@@ -270,20 +365,34 @@
         cross[j] = before + jnp.where(core == 0, total[h], 0.0)
         cross_copy(j).start()
 
-    halo_copy(0).wait_recv()
-    halo_copy(1).wait_recv()
-    band_first = band & ((col >= HD) | (ctx > 0))
-
-    @pl.loop(0, heads)
-    def _(h):
-        columns = pl.ds(pl.multiple_of(h * HD, HD), HD)
-        k_high, k_low = split(halo[0, :, columns])
-        v_high, v_low = split(halo[1, :, columns])
-        k2[h, :HD, :HD] = k_high
-        k2[h, :HD, HD:] = k_low
-        v2[h, :HD, :HD] = v_high
-        v2[h, :HD, HD:] = v_low
-        b_buf[h, :HD, :] = block(h, 0, band_first, causal_even)
+    def cross_done():
+        @pl.loop(0, half)
+        def _(j):
+            cross_copy(j).wait_send()
+
+    sent.append(cross_done)
+
+    def merge():
+        for g in range(groups):
+            answer_copy(g).wait_recv()
+        told_copy().wait_recv()
+        peak = own_peak[...]
+        other_peak = jnp.where(ctx > 0, heard[...], -3e38)
+        other_sum = pltpu.roll(heard[...], HD - heads, 1)
+        biggest = jnp.maximum(peak, other_peak)
+        scale = jnp.exp((peak - biggest) * factor)
+        other_scale = jnp.where(ctx > 0, jnp.exp((other_peak - biggest) * factor), 0.0)
+        whole = own_sum[...] * scale + other_sum * other_scale
+        scale = scale / whole
+        other_scale = other_scale / whole
+        square = acc_a[:HD, :]
+        for h in range(heads):
+            columns = slice(h % 2 * HD, (h % 2 + 1) * HD)
+            a = a_buf[h, :HD, :] * scale[:, h : h + 1]
+            a = (a + answered[h // 2, :, columns] * other_scale[:, h : h + 1]) * gain[0, h]
+            a_buf[h, :HD, :] = a
+            square = square + a * a
+        acc_a[:HD, :] = square
 
     def last_linear(h):
         r = dot(q2[h], wide(state[h]), 1, 0)
@@ -299,6 +408,8 @@
     def _(j):
         cross_copy(j).wait_recv()
         last_linear(half * (1 - core) + j)
+
+    merge()
 
     sums = []
     for acc in (acc_a, acc_b):
@@ -321,6 +432,7 @@
 
     for d in range(1, head_axis):
         z_copy(d, z).start()
+        sent.append(z_copy(d, z).wait_send)
     for d in range(1, head_axis):
         z_copy(d, lax.rem(z + d, head_axis)).wait_recv()
     squares = zbuf[0]
@@ -336,23 +448,8 @@
         for h in range(heads):
             out[here, h * HD : (h + 1) * HD] = a_buf[h, here, :] * scale_a + b_buf[h, here, :] * scale_b
 
-    for slot in range(2):
-        halo_copy(slot).wait_send()
-    for d in range(1, head_axis):
-        z_copy(d, z).wait_send()
-
-    @pl.loop(0, half)
-    def _(j):
-        pair_copy(j).wait_send()
-        cross_copy(j).wait_send()
-        for i in range(per_head):
-            @pl.when(owner(j, i) != mine)
-            def _():
-                gather_copy(j, i, owner(j, i), mine).wait_send()
-
-    @pl.loop(1, chips)
-    def _(d):
-        prefix_copy(d, my_piece).wait_send()
+    for finish in sent:
+        finish()
 
 
 def shards(ctx_count, head_axis, queries, keys, values, head_gain):
@@ -369,16 +466,22 @@
     body = functools.partial(kernel, ctx_count, head_axis, heads, rows)
     return pl.pallas_call(
         body,
-        out_shape=jax.ShapeDtypeStruct((rows, heads * HD), F32),
+        out_shape=pltpu.VMEM((rows, heads * HD), F32),
         in_specs=[anywhere, anywhere, anywhere, pl.BlockSpec(memory_space=pltpu.SMEM)],
         out_specs=pl.BlockSpec(memory_space=pltpu.VMEM),
         scratch_shapes=[
             vmem((heads, rows, HD), F32),
             vmem((heads, rows, HD), F32),
             vmem((heads, rows, HD), F32),
-            vmem((2, HD, heads * HD), F32),
-            vmem((heads, rows + HD, 2 * HD), BF16),
-            vmem((heads, rows + HD, 2 * HD), BF16),
+            vmem((heads // 2, HD, 2 * HD), F32),
+            vmem((heads // 2, HD, 2 * HD), F32),
+            vmem((heads // 2, HD, 2 * HD), F32),
+            vmem((HD, HD), F32),
+            vmem((HD, HD), F32),
+            vmem((HD, HD), F32),
+            vmem((HD, HD), F32),
+            vmem((heads, rows, 2 * HD), BF16),
+            vmem((heads, rows, 2 * HD), BF16),
             vmem((heads, rows, 2 * HD), BF16),
             vmem((heads, HD, HD), F32),
             vmem((heads, HD, HD), F32),
@@ -396,8 +499,12 @@
             vmem((2 * blocks, HD), F32),
             vmem((head_axis, 2 * blocks, HD), F32),
             dma((3, heads)),
-            dma((2,)),
-            dma((2,)),
+            dma((heads // 2,)),
+            dma((heads // 2,)),
+            dma((heads // 2,)),
+            dma((heads // 2,)),
+            dma,
+            dma,
             dma((half,)),
             dma((half,)),
             dma((half, per_head)),

time: 50.6 us -> 41.9 us (0.83)
  Pallas kernels: 47.3 us -> 40.5 us
  local copies, waits for them, and re-layouts: 3.16 us -> 1.32 us
    pallas_call x1, Pallas kernels: 47.3 us -> 40.5 us  [shards(): pl.pallas_call(body, out_shape=pltpu.VMEM((rows, heads * HD), F32), in_sp...]
    unnamed x1, local copies, waits for them, and re-layouts: 3.16 us -> 1.32 us
where the time goes in v2:
time: 41.9 us; the launch traced here: 41.8 us
  Pallas kernels  40.5 us (97%)
  local copies, waits for them, and re-layouts  1.32 us (3%)
    pallas_call x1, Pallas kernels, shards(): pl.pallas_call(body, out_shape=pltpu.VMEM((rows, heads * HD), F32), in_sp...  40.5 us
    unnamed x1, local copies, waits for them, and re-layouts  1.32 us

profile of v2, /device:TPU:1, one launch (start us, length us, event | category | flops | bytes accessed | tf_op | source)
XLA Modules:
  0.0 41.8 jit_solution(43897741809244163)
XLA Ops:
  0.0 40.5 %shard_map.46 = f32[512,1024]{1,0:T(8,128)S(1)} custom-call(f32[512,1024]{1,0:T(8,128)} %q_hbm.1, f32[512,1024]{1,0:T(8,128)} %k_hbm.1, f32[512,1024]{1,0:T(8,128)} %v_hbm.1, f32[2,8]{1,0:T(2,128)} %gain.1), custom_call_target="tpu_custom_call" | custom-call | tf_op jit(solution)/shard_map/pallas_call | solution.py:467
  40.5 1.3 %copy.6 = f32[512,1024]{1,0:T(8,128)} copy(f32[512,1024]{1,0:T(8,128)S(1)} %shard_map.46) | data formatting | bytes 4194304

commit v3 on v2

--- a/solution.py
+++ b/solution.py
@@ -12,6 +12,9 @@
 HD = 128
 WINDOW = 128
 MESH = pl.DeviceIdType.MESH
+PARTS = 2
+START = (("v", 0), ("q", 0), ("q", 1),)
+ORDER = (("q", 2), ("i", 0), ("i", 1), ("i", 2), ("i", 3), ("a", 0), ("p", 0), ("a", 1), ("i", 4), ("p", 1), ("i", 5), ("i", 6), ("a", 2), ("i", 7), ("k", 0), ("f", 0), ("f", 1), ("f", 2), ("f", 3),)
 F32 = jnp.float32
 BF16 = jnp.bfloat16
 
@@ -35,9 +38,9 @@
     ctx_count, head_axis, heads, rows,
     q_hbm, k_hbm, v_hbm, gain,
     out,
-    kbuf, vbuf, qbuf, asked, answer, answered, told, heard, own_peak, own_sum, k2, v2, q2, first, total, pair, chip, gather, prefix, piece_in, state, cross,
+    kbuf, vbuf, qbuf, asked, answer, answered, halo, told, heard, kept, own_peak, own_sum, k2, v2, q2, first, total, pair, chip, gather, prefix, piece_in, state, cross,
     a_buf, b_buf, acc_a, acc_b, zsend, zbuf,
-    load_sem, ask_send, ask_recv, answer_send, answer_recv, told_send, told_recv, pair_send, pair_recv, gather_send, gather_recv,
+    load_sem, halo_send, halo_recv, ask_send, ask_recv, answer_send, answer_recv, told_send, told_recv, pair_send, pair_recv, gather_send, gather_recv,
     prefix_send, prefix_recv, cross_send, cross_recv, z_send, z_recv,
 ):
     ctx = lax.axis_index("ctx")
@@ -46,26 +49,26 @@
     mine = lax.div(ctx, 2)
     chips = ctx_count // 2
     half = heads // 2
-    per_head = chips // half
-    depth = HD // per_head
+    each = half // PARTS
+    depth = each * HD // chips
     blocks = rows // HD
     factor = 1.0 / math.sqrt(HD)
     sibling = (ctx + 1 - 2 * core, z)
     following = (lax.rem(ctx + 1, ctx_count), z)
     preceding = (lax.rem(ctx + ctx_count - 1, ctx_count), z)
-    side = 4 if chips == 16 else 0
-
-    def owner(j, i):
-        if side:
-            return side * i + lax.rem(i + j, side)
-        return j * per_head + i
-
-    def piece_of(c):
-        if side:
-            y = lax.div(c, side)
-            x = lax.rem(c, side)
-            return side * lax.rem(x + side - y, side) + y
-        return c
+    side = math.isqrt(chips)
+    my_y, my_x = lax.div(mine, side), lax.rem(mine, side)
+    others = []
+    for dy in range(side):
+        for dx in range(side):
+            hops = min(dx, side - dx) + min(dy, side - dy)
+            if hops:
+                other = lax.rem(my_y + dy, side) * side + lax.rem(my_x + dx, side)
+                others.append((hops, len(others), other))
+    others = [other for _, _, other in sorted(others, key=lambda o: (-o[0], o[1]))]
+
+    def piece(c):
+        return pl.ds(pl.multiple_of(c * depth, depth), depth)
 
     def load(source, target, slot, h):
         columns = pl.ds(pl.multiple_of(h * HD, HD), HD)
@@ -85,13 +88,13 @@
     greet(following)
     greet(preceding)
     greet(sibling)
-    for d in range(1, chips):
-        greet((2 * lax.rem(mine + d, chips) + core, z))
+    for other in others:
+        greet((2 * other + core, z))
     for d in range(1, head_axis):
         greet((ctx, lax.rem(z + d, head_axis)))
     for h in range(heads):
         load(q_hbm, qbuf, 2, h).start()
-    groups = heads // 2
+    groups = heads // 2 - 1
     last = slice(rows - HD, rows)
 
     def ask_copy(g):
@@ -113,6 +116,25 @@
             device_id=following,
             device_id_type=MESH,
         )
+
+    kept_columns = pl.ds(groups * 2 * HD, 2 * HD)
+
+    def halo_copy(slot):
+        return pltpu.make_async_remote_copy(
+            src_ref=(k_hbm, v_hbm)[slot].at[pl.ds(rows - HD, HD), kept_columns],
+            dst_ref=halo.at[slot],
+            send_sem=halo_send.at[slot],
+            recv_sem=halo_recv.at[slot],
+            device_id=following,
+            device_id_type=MESH,
+        )
+
+    def send_halo(_):
+        for slot in range(2):
+            halo_copy(slot).start()
+
+    def ask(g):
+        ask_copy(g).start()
 
     def told_copy():
         return pltpu.make_async_remote_copy(
@@ -153,15 +175,29 @@
             device_id_type=MESH,
         )
 
-    def gather_copy(j, i, target, slot):
-        return pltpu.make_async_remote_copy(
-            src_ref=chip.at[j, pl.ds(i * depth, depth), :],
-            dst_ref=gather.at[slot],
-            send_sem=gather_send.at[j, i],
-            recv_sem=gather_recv.at[slot],
+    def gather_copy(j, target):
+        return pltpu.make_async_remote_copy(
+            src_ref=chip.at[j, piece(target), :],
+            dst_ref=gather.at[j, mine],
+            send_sem=gather_send.at[j],
+            recv_sem=gather_recv.at[j],
             device_id=(2 * target + core, z),
             device_id_type=MESH,
         )
+
+    def prefix_copy(j, target):
+        return pltpu.make_async_remote_copy(
+            src_ref=prefix.at[j, target],
+            dst_ref=piece_in.at[j, piece(mine), :],
+            send_sem=prefix_send.at[j],
+            recv_sem=prefix_recv.at[j],
+            device_id=(2 * target + core, z),
+            device_id_type=MESH,
+        )
+
+    def all_others(semaphore):
+        sample = gather.at[0, pl.ds(0, chips - 1)]
+        pltpu.make_async_copy(sample, sample, semaphore).wait()
 
     @pl.loop(0, half)
     def _(j):
@@ -170,9 +206,12 @@
     pl.semaphore_wait(barrier, 3 + chips - 1 + head_axis - 1)
     for j in range(half):
         pair_copy(j).start()
+    for name, which in START:
+        {"v": send_halo, "q": ask}[name](which)
     for g in range(groups):
-        ask_copy(g).start()
         sent.append(ask_copy(g).wait_send)
+    for slot in range(2):
+        sent.append(halo_copy(slot).wait_send)
 
     def pair_done():
         @pl.loop(0, half)
@@ -181,33 +220,24 @@
 
     sent.append(pair_done)
 
-    @pl.loop(0, half)
-    def _(j):
-        h = half * core + j
-        local_state(h)
-        pair_copy(j).wait_recv()
-        chip[j] = total[h] + pair[j]
-        for i in range(per_head):
-            target = owner(j, i)
-
-            @pl.when(target == mine)
-            def _():
-                gather[mine] = chip[j, i * depth : (i + 1) * depth, :]
-
-            @pl.when(target != mine)
-            def _():
-                gather_copy(j, i, target, mine).start()
+    @pl.loop(0, PARTS)
+    def _(p):
+        for e in range(each):
+            j = p * each + e
+            h = half * core + j
+            local_state(h)
+            pair_copy(j).wait_recv()
+            chip[p, e * HD : (e + 1) * HD, :] = total[h] + pair[j]
+        gather[p, mine] = chip[p, piece(mine), :]
+        for other in others:
+            gather_copy(p, other).start()
 
     def gather_done():
-        @pl.loop(0, half)
-        def _(j):
-            for i in range(per_head):
-                @pl.when(owner(j, i) != mine)
-                def _():
-                    gather_copy(j, i, owner(j, i), mine).wait_send()
+        @pl.loop(0, PARTS)
+        def _(p):
+            all_others(gather_send.at[p])
 
     sent.append(gather_done)
-
     row = lax.broadcasted_iota(jnp.int32, (HD, 2 * HD), 0)
     col = lax.broadcasted_iota(jnp.int32, (HD, 2 * HD), 1)
     band = (col > row) & (col <= row + HD)
@@ -219,6 +249,7 @@
     acc_a[...] = jnp.zeros_like(acc_a)
     acc_b[...] = jnp.zeros_like(acc_b)
     told[...] = jnp.zeros_like(told)
+    kept[...] = jnp.zeros_like(kept)
     own_peak[...] = jnp.zeros_like(own_peak)
     own_sum[...] = jnp.zeros_like(own_sum)
 
@@ -264,81 +295,49 @@
                 lin = lin + carried[n * HD - mid : (n + 1) * HD - mid]
             b_buf[h, n * HD : (n + 1) * HD, :] = lin
 
+    def partial(h, q_high, q_low, keys, vals, target, tile):
+        s = scores(jnp.concatenate([q_low, q_high], axis=1), keys)
+        biggest = jnp.max(jnp.where(lower, -3e38, s), axis=1, keepdims=True)
+        weights = jnp.where(lower, 0.0, jnp.exp((s - biggest) * factor))
+        weight_sum = jnp.sum(weights, axis=1, keepdims=True)
+        r = dot(jnp.concatenate(split(weights), axis=0), vals, 1, 0)
+        target[:, h % 2 * HD : (h % 2 + 1) * HD] = r[:HD, :HD] + (r[:HD, HD:] + r[HD:, :HD])
+        tile[...] = jnp.where(lane == h, biggest, jnp.where(lane == heads + h, weight_sum, tile[...]))
+
     def answer_group(g):
         ask_copy(g).wait_recv()
-        for e in range(2):
-            h = 2 * g + e
-            columns = slice(e * HD, (e + 1) * HD)
-            q_high, q_low = split(asked[g, :, columns])
-            s = scores(jnp.concatenate([q_low, q_high], axis=1), k2[h, last, :])
-            biggest = jnp.max(jnp.where(lower, -3e38, s), axis=1, keepdims=True)
-            weights = jnp.where(lower, 0.0, jnp.exp((s - biggest) * factor))
-            weight_sum = jnp.sum(weights, axis=1, keepdims=True)
-            r = dot(jnp.concatenate(split(weights), axis=0), v2[h, last, :], 1, 0)
-            answer[g, :, columns] = r[:HD, :HD] + (r[:HD, HD:] + r[HD:, :HD])
-            told[...] = jnp.where(
-                lane == h, biggest, jnp.where(lane == heads + h, weight_sum, told[...])
-            )
+        for h in (2 * g, 2 * g + 1):
+            q_high, q_low = split(asked[g, :, h % 2 * HD : (h % 2 + 1) * HD])
+            partial(h, q_high, q_low, k2[h, last, :], v2[h, last, :], answer.at[g], told)
         answer_copy(g).start()
 
-    early = heads - groups - 2
-
-    @pl.loop(0, early)
-    def _(h):
-        inner_blocks(h)
-
-    @pl.loop(0, groups)
-    def _(g):
-        answer_group(g)
-        inner_blocks(early + g)
-
-    def answer_done():
-        @pl.loop(0, groups)
-        def _(g):
-            answer_copy(g).wait_send()
-
-        told_copy().wait_send()
-
-    told_copy().start()
-    sent.append(answer_done)
-
-    def prefix_copy(d, slot):
-        target = lax.rem(mine + d, chips)
-        return pltpu.make_async_remote_copy(
-            src_ref=prefix.at[target],
-            dst_ref=piece_in.at[slot],
-            send_sem=prefix_send.at[d],
-            recv_sem=prefix_recv.at[slot],
-            device_id=(2 * target + core, z),
-            device_id_type=MESH,
-        )
-
-    @pl.loop(1, chips)
-    def _(d):
-        gather_copy(0, 0, mine, lax.rem(mine + d, chips)).wait_recv()
-
-    running = jnp.zeros((depth, HD), F32)
-    for c in range(chips):
-        prefix[c] = running
-        if c < chips - 1:
-            running = running + gather[c]
-    my_piece = piece_of(mine)
-    piece_in[my_piece] = prefix[mine]
-
-    @pl.loop(1, chips)
-    def _(d):
-        prefix_copy(d, my_piece).start()
+    def keep_group(_):
+        for slot in range(2):
+            halo_copy(slot).wait_recv()
+        for h in (2 * groups, 2 * groups + 1):
+            columns = slice(h % 2 * HD, (h % 2 + 1) * HD)
+            keys = jnp.concatenate(split(halo[0, :, columns]), axis=1)
+            vals = jnp.concatenate(split(halo[1, :, columns]), axis=1)
+            q_low_high = q2[h, :HD, :]
+            partial(h, q_low_high[:, HD:], q_low_high[:, :HD], keys, vals, answered.at[groups], kept)
+
+    def return_prefixes(j):
+        all_others(gather_recv.at[j])
+        running = jnp.zeros((depth, HD), F32)
+        for c in range(chips):
+            prefix[j, c] = running
+            if c < chips - 1:
+                running = running + gather[j, c]
+        piece_in[j, piece(mine), :] = prefix[j, mine]
+        for other in others:
+            prefix_copy(j, other).start()
 
     def prefix_done():
-        @pl.loop(1, chips)
-        def _(d):
-            prefix_copy(d, my_piece).wait_send()
+        @pl.loop(0, PARTS)
+        def _(p):
+            all_others(prefix_send.at[p])
 
     sent.append(prefix_done)
-
-    @pl.loop(early + groups, heads)
-    def _(h):
-        inner_blocks(h)
 
     def cross_copy(j):
         return pltpu.make_async_remote_copy(
@@ -350,20 +349,24 @@
             device_id_type=MESH,
         )
 
-    @pl.loop(0, half)
-    def _(j):
+    def forward(j):
         h = half * core + j
-        for i in range(per_head):
-            p = j * per_head + i
-
-            @pl.when(p != my_piece)
-            def _():
-                prefix_copy(1, p).wait_recv()
-
-        before = piece_in[pl.ds(j * per_head, per_head)].reshape(HD, HD)
+        p, e = j // each, j % each
+        if e == 0:
+            all_others(prefix_recv.at[p])
+        before = piece_in[p, e * HD : (e + 1) * HD, :]
         state[h] = before + jnp.where(core == 1, pair[j], 0.0)
         cross[j] = before + jnp.where(core == 0, total[h], 0.0)
         cross_copy(j).start()
+
+    def inner_pair(h):
+        @pl.loop(h, h + 2)
+        def _(each):
+            inner_blocks(each)
+
+    steps = {"v": send_halo, "k": keep_group, "q": ask, "i": inner_blocks, "d": inner_pair, "a": answer_group, "p": return_prefixes, "f": forward}
+    for name, which in ORDER:
+        steps[name](which)
 
     def cross_done():
         @pl.loop(0, half)
@@ -371,14 +374,25 @@
             cross_copy(j).wait_send()
 
     sent.append(cross_done)
+
+    def answer_done():
+        @pl.loop(0, groups)
+        def _(g):
+            answer_copy(g).wait_send()
+
+        told_copy().wait_send()
+
+    told_copy().start()
+    sent.append(answer_done)
 
     def merge():
         for g in range(groups):
             answer_copy(g).wait_recv()
         told_copy().wait_recv()
         peak = own_peak[...]
-        other_peak = jnp.where(ctx > 0, heard[...], -3e38)
-        other_sum = pltpu.roll(heard[...], HD - heads, 1)
+        other = heard[...] + kept[...]
+        other_peak = jnp.where(ctx > 0, other, -3e38)
+        other_sum = pltpu.roll(other, HD - heads, 1)
         biggest = jnp.maximum(peak, other_peak)
         scale = jnp.exp((peak - biggest) * factor)
         other_scale = jnp.where(ctx > 0, jnp.exp((other_peak - biggest) * factor), 0.0)
@@ -404,37 +418,42 @@
     def _(j):
         last_linear(half * core + j)
 
+    merge()
+
+    def block_sums(acc):
+        turned = [jnp.transpose(acc[n * HD : (n + 1) * HD, :]) for n in range(blocks)]
+        return [jnp.sum(t, axis=0, keepdims=True) for t in turned]
+
+    sums = block_sums(acc_a)
+
     @pl.loop(0, half)
     def _(j):
         cross_copy(j).wait_recv()
         last_linear(half * (1 - core) + j)
 
-    merge()
-
-    sums = []
-    for acc in (acc_a, acc_b):
-        for n in range(blocks):
-            turned = jnp.transpose(acc[n * HD : (n + 1) * HD, :])
-            sums.append(jnp.sum(turned, axis=0, keepdims=True))
+    sums = sums + block_sums(acc_b)
     sums = jnp.concatenate(sums, axis=0)
     zsend[...] = sums
     zbuf[z] = sums
 
-    def z_copy(d, slot):
+    def z_copy(d):
         return pltpu.make_async_remote_copy(
             src_ref=zsend,
-            dst_ref=zbuf.at[slot],
-            send_sem=z_send.at[d],
-            recv_sem=z_recv.at[slot],
+            dst_ref=zbuf.at[z],
+            send_sem=z_send,
+            recv_sem=z_recv,
             device_id=(ctx, lax.rem(z + d, head_axis)),
             device_id_type=MESH,
         )
 
-    for d in range(1, head_axis):
-        z_copy(d, z).start()
-        sent.append(z_copy(d, z).wait_send)
-    for d in range(1, head_axis):
-        z_copy(d, lax.rem(z + d, head_axis)).wait_recv()
+    def z_wait(semaphore):
+        sample = zbuf.at[pl.ds(0, head_axis - 1)]
+        pltpu.make_async_copy(sample, sample, semaphore).wait()
+
+    for d in sorted(range(1, head_axis), key=lambda d: -min(d, head_axis - d)):
+        z_copy(d).start()
+    sent.append(lambda: z_wait(z_send))
+    z_wait(z_recv)
     squares = zbuf[0]
     for other in range(1, head_axis):
         squares = squares + zbuf[other]
@@ -457,8 +476,8 @@
     heads = head_gain.shape[1]
     chips = ctx_count // 2
     half = heads // 2
-    depth = half * HD // chips
-    per_head = chips // half
+    each = half // PARTS
+    depth = each * HD // chips
     blocks = rows // HD
     anywhere = pl.BlockSpec(memory_space=pl.ANY)
     dma = pltpu.SemaphoreType.DMA
@@ -473,9 +492,11 @@
             vmem((heads, rows, HD), F32),
             vmem((heads, rows, HD), F32),
             vmem((heads, rows, HD), F32),
+            vmem((heads // 2 - 1, HD, 2 * HD), F32),
+            vmem((heads // 2 - 1, HD, 2 * HD), F32),
             vmem((heads // 2, HD, 2 * HD), F32),
-            vmem((heads // 2, HD, 2 * HD), F32),
-            vmem((heads // 2, HD, 2 * HD), F32),
+            vmem((2, HD, 2 * HD), F32),
+            vmem((HD, HD), F32),
             vmem((HD, HD), F32),
             vmem((HD, HD), F32),
             vmem((HD, HD), F32),
@@ -486,10 +507,10 @@
             vmem((heads, HD, HD), F32),
             vmem((heads, HD, HD), F32),
             vmem((half, HD, HD), F32),
-            vmem((half, HD, HD), F32),
-            vmem((chips, depth, HD), F32),
-            vmem((chips, depth, HD), F32),
-            vmem((chips, depth, HD), F32),
+            vmem((PARTS, each * HD, HD), F32),
+            vmem((PARTS, chips, depth, HD), F32),
+            vmem((PARTS, chips, depth, HD), F32),
+            vmem((PARTS, each * HD, HD), F32),
             vmem((heads, HD, HD), F32),
             vmem((half, HD, HD), F32),
             vmem((heads, rows, HD), F32),
@@ -499,6 +520,8 @@
             vmem((2 * blocks, HD), F32),
             vmem((head_axis, 2 * blocks, HD), F32),
             dma((3, heads)),
+            dma((2,)),
+            dma((2,)),
             dma((heads // 2,)),
             dma((heads // 2,)),
             dma((heads // 2,)),
@@ -507,14 +530,14 @@
             dma,
             dma((half,)),
             dma((half,)),
-            dma((half, per_head)),
-            dma((chips,)),
-            dma((chips,)),
-            dma((chips,)),
+            dma((PARTS,)),
+            dma((PARTS,)),
+            dma((PARTS,)),
+            dma((PARTS,)),
             dma((half,)),
             dma((half,)),
-            dma((head_axis,)),
-            dma((head_axis,)),
+            dma,
+            dma,
         ],
         compiler_params=pltpu.CompilerParams(
             collective_id=0, has_side_effects=True, vmem_limit_bytes=60 * 1024 * 1024

time: 41.9 us -> 38.1 us (0.909)
  the two profiles are of different devices: /device:TPU:1 before, /device:TPU:32 now
where the time goes in v3:
time: 38.1 us; the launch traced here: 38 us
  Pallas kernels  36.7 us (96%)
  local copies, waits for them, and re-layouts  1.32 us (3%)
    pallas_call x1, Pallas kernels, shards(): pl.pallas_call(body, out_shape=pltpu.VMEM((rows, heads * HD), F32), in_sp...  36.7 us
    unnamed x1, local copies, waits for them, and re-layouts  1.32 us

profile of v3, /device:TPU:32, one launch (start us, length us, event | category | flops | bytes accessed | tf_op | source)
XLA Modules:
  0.0 38.0 jit_solution(11424874867783455800)
XLA Ops:
  0.0 36.7 %shard_map.46 = f32[512,1024]{1,0:T(8,128)S(1)} custom-call(f32[512,1024]{1,0:T(8,128)} %q_hbm.1, f32[512,1024]{1,0:T(8,128)} %k_hbm.1, f32[512,1024]{1,0:T(8,128)} %v_hbm.1, f32[2,8]{1,0:T(2,128)} %gain.1), custom_call_target="tpu_custom_call" | custom-call | tf_op jit(solution)/shard_map/pallas_call | solution.py:486
  36.7 1.3 %copy.6 = f32[512,1024]{1,0:T(8,128)} copy(f32[512,1024]{1,0:T(8,128)S(1)} %shard_map.46) | data formatting | bytes 4194304

commit v4 on v3

--- a/solution.py
+++ b/solution.py
@@ -14,7 +14,7 @@
 MESH = pl.DeviceIdType.MESH
 PARTS = 2
 START = (("v", 0), ("q", 0), ("q", 1),)
-ORDER = (("q", 2), ("i", 0), ("i", 1), ("i", 2), ("i", 3), ("a", 0), ("p", 0), ("a", 1), ("i", 4), ("p", 1), ("i", 5), ("i", 6), ("a", 2), ("i", 7), ("k", 0), ("f", 0), ("f", 1), ("f", 2), ("f", 3),)
+ORDER = (("q", 2), ("i", 0), ("i", 1), ("i", 2), ("i", 3), ("p", 0), ("a", 0), ("i", 4), ("p", 1), ("a", 1), ("i", 5), ("a", 2), ("i", 6), ("i", 7), ("k", 0), ("f", 0), ("f", 1), ("f", 2), ("f", 3),)
 F32 = jnp.float32
 BF16 = jnp.bfloat16
 
@@ -75,6 +75,15 @@
         return pltpu.make_async_copy(source.at[:, columns], target.at[h], load_sem.at[slot, h])
 
     sent = []
+    has_before = ctx > 0
+    has_after = ctx < ctx_count - 1
+
+    def when(condition, *actions):
+        @pl.when(condition)
+        def _():
+            for action in actions:
+                action()
+
 
     barrier = pltpu.get_barrier_semaphore()
 
@@ -130,11 +139,10 @@
         )
 
     def send_halo(_):
-        for slot in range(2):
-            halo_copy(slot).start()
+        when(has_after, *[halo_copy(slot).start for slot in range(2)])
 
     def ask(g):
-        ask_copy(g).start()
+        when(has_before, ask_copy(g).start)
 
     def told_copy():
         return pltpu.make_async_remote_copy(
@@ -208,10 +216,8 @@
         pair_copy(j).start()
     for name, which in START:
         {"v": send_halo, "q": ask}[name](which)
-    for g in range(groups):
-        sent.append(ask_copy(g).wait_send)
-    for slot in range(2):
-        sent.append(halo_copy(slot).wait_send)
+    sent.append(lambda: when(has_before, *[ask_copy(g).wait_send for g in range(groups)]))
+    sent.append(lambda: when(has_after, *[halo_copy(slot).wait_send for slot in range(2)]))
 
     def pair_done():
         @pl.loop(0, half)
@@ -251,6 +257,17 @@
     told[...] = jnp.zeros_like(told)
     kept[...] = jnp.zeros_like(kept)
     own_peak[...] = jnp.zeros_like(own_peak)
+
+    @pl.when(ctx == 0)
+    def _():
+        answered[...] = jnp.zeros_like(answered)
+        heard[...] = jnp.zeros_like(heard)
+        halo[...] = jnp.zeros_like(halo)
+
+    @pl.when(ctx == ctx_count - 1)
+    def _():
+        asked[...] = jnp.zeros_like(asked)
+
     own_sum[...] = jnp.zeros_like(own_sum)
 
     def scores(q_low_high, keys):
@@ -305,15 +322,14 @@
         tile[...] = jnp.where(lane == h, biggest, jnp.where(lane == heads + h, weight_sum, tile[...]))
 
     def answer_group(g):
-        ask_copy(g).wait_recv()
+        when(has_after, ask_copy(g).wait_recv)
         for h in (2 * g, 2 * g + 1):
             q_high, q_low = split(asked[g, :, h % 2 * HD : (h % 2 + 1) * HD])
             partial(h, q_high, q_low, k2[h, last, :], v2[h, last, :], answer.at[g], told)
-        answer_copy(g).start()
+        when(has_after, answer_copy(g).start)
 
     def keep_group(_):
-        for slot in range(2):
-            halo_copy(slot).wait_recv()
+        when(has_before, *[halo_copy(slot).wait_recv for slot in range(2)])
         for h in (2 * groups, 2 * groups + 1):
             columns = slice(h % 2 * HD, (h % 2 + 1) * HD)
             keys = jnp.concatenate(split(halo[0, :, columns]), axis=1)
@@ -376,19 +392,13 @@
     sent.append(cross_done)
 
     def answer_done():
-        @pl.loop(0, groups)
-        def _(g):
-            answer_copy(g).wait_send()
-
-        told_copy().wait_send()
-
-    told_copy().start()
+        when(has_after, told_copy().wait_send, *[answer_copy(g).wait_send for g in range(groups)])
+
+    when(has_after, told_copy().start)
     sent.append(answer_done)
 
     def merge():
-        for g in range(groups):
-            answer_copy(g).wait_recv()
-        told_copy().wait_recv()
+        when(has_before, told_copy().wait_recv, *[answer_copy(g).wait_recv for g in range(groups)])
         peak = own_peak[...]
         other = heard[...] + kept[...]
         other_peak = jnp.where(ctx > 0, other, -3e38)

time: 38.1 us -> 37.3 us (0.979)
  the two profiles are of different devices: /device:TPU:32 before, /device:TPU:8 now
where the time goes in v4:
time: 37.3 us; the launch traced here: 37.2 us
  Pallas kernels  35.9 us (96%)
  local copies, waits for them, and re-layouts  1.32 us (4%)
    pallas_call x1, Pallas kernels, shards(): pl.pallas_call(body, out_shape=pltpu.VMEM((rows, heads * HD), F32), in_sp...  35.9 us
    unnamed x1, local copies, waits for them, and re-layouts  1.32 us

profile of v4, /device:TPU:8, one launch (start us, length us, event | category | flops | bytes accessed | tf_op | source)
XLA Modules:
  0.0 37.2 jit_solution(15873732482823089213)
XLA Ops:
  0.0 35.9 %shard_map.46 = f32[512,1024]{1,0:T(8,128)S(1)} custom-call(f32[512,1024]{1,0:T(8,128)} %q_hbm.1, f32[512,1024]{1,0:T(8,128)} %k_hbm.1, f32[512,1024]{1,0:T(8,128)} %v_hbm.1, f32[2,8]{1,0:T(2,128)} %gain.1), custom_call_target="tpu_custom_call" | custom-call | tf_op jit(solution)/shard_map/pallas_call | solution.py:496
  35.9 1.3 %copy.6 = f32[512,1024]{1,0:T(8,128)} copy(f32[512,1024]{1,0:T(8,128)S(1)} %shard_map.46) | data formatting | bytes 4194304

commit v5 on v4

--- a/solution.py
+++ b/solution.py
@@ -428,22 +428,19 @@
     def _(j):
         last_linear(half * core + j)
 
-    merge()
-
-    def block_sums(acc):
-        turned = [jnp.transpose(acc[n * HD : (n + 1) * HD, :]) for n in range(blocks)]
-        return [jnp.sum(t, axis=0, keepdims=True) for t in turned]
-
-    sums = block_sums(acc_a)
-
     @pl.loop(0, half)
     def _(j):
         cross_copy(j).wait_recv()
         last_linear(half * (1 - core) + j)
 
-    sums = sums + block_sums(acc_b)
-    sums = jnp.concatenate(sums, axis=0)
-    zsend[...] = sums
+    def block_sum(acc, n):
+        return jnp.sum(jnp.transpose(acc[n * HD : (n + 1) * HD, :]), axis=0, keepdims=True)
+
+    sums = [block_sum(acc_a, n) for n in range(1, blocks)] + [block_sum(acc_b, n) for n in range(blocks)]
+    zsend[1:, :] = jnp.concatenate(sums, axis=0)
+    merge()
+    zsend[:1, :] = block_sum(acc_a, 0)
+    sums = zsend[...]
     zbuf[z] = sums
 
     def z_copy(d):

time: 37.3 us -> 36.2 us (0.971)
  Pallas kernels: 35.9 us -> 34.8 us
    pallas_call x1, Pallas kernels: 35.9 us -> 34.8 us  [shards(): pl.pallas_call(body, out_shape=pltpu.VMEM((rows, heads * HD), F32), in_sp...]
where the time goes in v5:
time: 36.2 us; the launch traced here: 36.1 us
  Pallas kernels  34.8 us (96%)
  local copies, waits for them, and re-layouts  1.32 us (4%)
    pallas_call x1, Pallas kernels, shards(): pl.pallas_call(body, out_shape=pltpu.VMEM((rows, heads * HD), F32), in_sp...  34.8 us
    unnamed x1, local copies, waits for them, and re-layouts  1.32 us

profile of v5, /device:TPU:8, one launch (start us, length us, event | category | flops | bytes accessed | tf_op | source)
XLA Modules:
  0.0 36.1 jit_solution(7506458332156137487)
XLA Ops:
  0.0 34.8 %shard_map.46 = f32[512,1024]{1,0:T(8,128)S(1)} custom-call(f32[512,1024]{1,0:T(8,128)} %q_hbm.1, f32[512,1024]{1,0:T(8,128)} %k_hbm.1, f32[512,1024]{1,0:T(8,128)} %v_hbm.1, f32[2,8]{1,0:T(2,128)} %gain.1), custom_call_target="tpu_custom_call" | custom-call | tf_op jit(solution)/shard_map/pallas_call | solution.py:493
  34.8 1.3 %copy.6 = f32[512,1024]{1,0:T(8,128)} copy(f32[512,1024]{1,0:T(8,128)S(1)} %shard_map.46) | data formatting | bytes 4194304

commit v6 on v5

--- a/solution.py
+++ b/solution.py
@@ -14,7 +14,7 @@
 MESH = pl.DeviceIdType.MESH
 PARTS = 2
 START = (("v", 0), ("q", 0), ("q", 1),)
-ORDER = (("q", 2), ("i", 0), ("i", 1), ("i", 2), ("i", 3), ("p", 0), ("a", 0), ("i", 4), ("p", 1), ("a", 1), ("i", 5), ("a", 2), ("i", 6), ("i", 7), ("k", 0), ("f", 0), ("f", 1), ("f", 2), ("f", 3),)
+ORDER = (("q", 2), ("i", 0), ("i", 1), ("i", 2), ("i", 3), ("p", 0), ("a", 0), ("i", 4), ("p", 1), ("a", 1), ("a", 2), ("i", 5), ("i", 6), ("i", 7), ("k", 0), ("f", 0), ("f", 1), ("f", 2), ("f", 3),)
 F32 = jnp.float32
 BF16 = jnp.bfloat16
 

time: 36.2 us -> 36.8 us (1.017)
  Pallas kernels: 34.8 us -> 35.4 us
    pallas_call x1, Pallas kernels: 34.8 us -> 35.4 us  [shards(): pl.pallas_call(body, out_shape=pltpu.VMEM((rows, heads * HD), F32), in_sp...]
where the time goes in v6:
time: 36.8 us; the launch traced here: 36.7 us
  Pallas kernels  35.4 us (96%)
  local copies, waits for them, and re-layouts  1.32 us (4%)
    pallas_call x1, Pallas kernels, shards(): pl.pallas_call(body, out_shape=pltpu.VMEM((rows, heads * HD), F32), in_sp...  35.4 us
    unnamed x1, local copies, waits for them, and re-layouts  1.32 us

profile of v6, /device:TPU:8, one launch (start us, length us, event | category | flops | bytes accessed | tf_op | source)
XLA Modules:
  0.0 36.7 jit_solution(14690221792495205300)
XLA Ops:
  0.0 35.4 %shard_map.46 = f32[512,1024]{1,0:T(8,128)S(1)} custom-call(f32[512,1024]{1,0:T(8,128)} %q_hbm.1, f32[512,1024]{1,0:T(8,128)} %k_hbm.1, f32[512,1024]{1,0:T(8,128)} %v_hbm.1, f32[2,8]{1,0:T(2,128)} %gain.1), custom_call_target="tpu_custom_call" | custom-call | tf_op jit(solution)/shard_map/pallas_call | solution.py:493
  35.4 1.3 %copy.6 = f32[512,1024]{1,0:T(8,128)} copy(f32[512,1024]{1,0:T(8,128)S(1)} %shard_map.46) | data formatting | bytes 4194304
